TPU v7x, 32 devices: a whole 2x2x4 slice. The times are simulated.
32 devices in a mesh: groups: 2 (over y), space: 4 (over z), batch: 4 (over x, core).
Axes of the slice: x: 2, y: 2, z: 4, core: 2. Of those that a mesh axis runs over, the one named last changes fastest.
Arguments:
- fields: bfloat16 [8, 32, 64, 128], P(('groups', 'batch'), 'space'), parts along dimension 0, may hold values from -36 to 36
- land: int32 [32, 64], P('space'), may hold values 0 or 1
- conv_in: bfloat16 [9, 128, 128], replicated, may hold values from -0.1875 to 0.1875
- conv_out: bfloat16 [9, 128, 128], replicated, may hold values from -0.1875 to 0.1875
- batchnorm_gain: float32 [128], replicated, may hold values from 0.25 to 1.75
- batchnorm_offset: float32 [128], replicated, may hold values from -3 to 3
- target_grad: bfloat16 [8, 32, 64, 128], P(('groups', 'batch'), 'space'), parts along dimension 0, may hold values from -6 to 6
Outputs:
- output: bfloat16 [8, 32, 64, 128], P(('groups', 'batch'), 'space'), parts along dimension 0
- grad_in: float32 [18, 128, 128], P('groups', None, 'batch'), parts along dimension 0
- grad_out: float32 [18, 128, 128], P('groups', None, 'batch'), parts along dimension 0
- gain_gradient: float32 [256], P('groups'), parts along dimension 0
- offset_gradient: float32 [256], P('groups'), parts along dimension 0
There are 2 independent parts, one for each index of `groups`. A program takes and returns all parts, laid end to end along the dimension named above; an argument that names none is the same for every part. Nothing has to cross between parts.
All inputs are finite; a program needn't handle non-finite values. No bound on the sum of `land` on one device may be relied on, other than what follows from the above.
Results may differ from a plain program's by a relative error of at most 0.025.
Values may be sent and summed in bfloat16 or wider, within the bound.
No kernel may reach another device: no remote copies, remote signals or barrier semaphores. Data moves between devices by JAX's collectives and lax.ppermute only.
A program may use at most 64 MiB of HBM per device.

v0:
```python
import jax
import jax.numpy as jnp
from jax import lax
from jax.sharding import PartitionSpec as P


def partner(value, axis, distance):
    mask = 2**distance
    pairs = [(source, source ^ mask) for source in range(lax.axis_size(axis))]
    return lax.ppermute(value, axis, pairs)


def extended_2(x, sides, width):
    for axis, dim in sides:
        size, length = (lax.axis_size(axis), x.shape[dim])
        up = [(i, (i + 1) % size) for i in range(size)]
        down = [(j, i) for i, j in up]
        last = lax.slice_in_dim(x, length - width, length, axis=dim)
        initial = lax.slice_in_dim(x, 0, width, axis=dim)
        before = lax.ppermute(last, axis, up)
        after = lax.ppermute(initial, axis, down)
        x = jnp.concatenate([before, x, after], axis=dim)
    return x


def mirror_row(row_part):
    steps_total = lax.axis_size("space").bit_length() - 1
    moved = row_part
    for bit_number in range(steps_total):
        moved = partner(moved, "space", bit_number)
    return jnp.flip(moved, axis=1)


def surround(field):
    ghost = mirror_row(field[:, :, -1, :])
    south = jnp.zeros_like(field[:, :, :1, :])
    extended = jnp.concatenate([south, field, ghost[:, :, None, :]], axis=2)
    return extended_2(extended, (("space", 1),), 1)


def convolve(padded, weights, lon, lat):
    chans = padded.shape[3]
    total = jnp.zeros((padded.shape[0] * lon * lat, weights.shape[2]), jnp.float32)
    for tap in range(9):
        first, second = (tap // 3, tap % 3)
        piece = padded[:, first : first + lon, second : second + lat, :].reshape(-1, chans)
        total = total + jnp.dot(piece, weights[tap], preferred_element_type=jnp.float32)
    return total.reshape(padded.shape[0], lon, lat, weights.shape[2])


def adjoint_conv(padded, weights, lon, lat):
    chans = padded.shape[3]
    ghost_row = padded[:, :, lat + 1, :]
    cleared = padded.at[:, :, lat + 1, :].set(jnp.zeros_like(ghost_row))
    total = jnp.zeros((padded.shape[0] * lon * lat, weights.shape[1]), jnp.float32)
    for tap in range(9):
        first, second = (tap // 3, tap % 3)
        piece = cleared[:, 2 - first : 2 - first + lon, 2 - second : 2 - second + lat, :].reshape(
            -1, chans
        )
        total = total + lax.dot_general(
            piece, weights[tap], (((1,), (1,)), ((), ())), preferred_element_type=jnp.float32
        )
    total = total.reshape(padded.shape[0], lon, lat, weights.shape[1])
    extra = jnp.zeros((padded.shape[0] * lon, weights.shape[1]), jnp.float32)
    for first in range(3):
        piece = ghost_row[:, first : first + lon, :].reshape(-1, chans)
        extra = extra + lax.dot_general(
            piece,
            weights[3 * first + 2],
            (((1,), (1,)), ((), ())),
            preferred_element_type=jnp.float32,
        )
    extra = extra.reshape(padded.shape[0], lon, weights.shape[1])
    return total.at[:, :, lat - 1, :].add(extra)


def tap_grads(padded, grad, lon, lat):
    chans = padded.shape[3]
    flat = grad.reshape(-1, grad.shape[3])
    result = []
    for tap in range(9):
        first, second = (tap // 3, tap % 3)
        piece = padded[:, first : first + lon, second : second + lat, :].reshape(-1, chans)
        result.append(
            lax.dot_general(
                piece, flat, (((0,), (0,)), ((), ())), preferred_element_type=jnp.float32
            )
        )
    return jnp.stack(result, axis=0)


def reduce_weights(partial_grad):
    summed = lax.psum(partial_grad.astype(jnp.bfloat16), "space")
    return lax.psum_scatter(summed, "batch", scatter_dimension=2, tiled=True).astype(jnp.float32)


def gelu_value(value):
    inner = 0.7978845608 * (value + 0.044715 * value * value * value)
    return 0.5 * value * (1.0 + jnp.tanh(inner))


def gelu_slope(value):
    inner = 0.7978845608 * (value + 0.044715 * value * value * value)
    hyper = jnp.tanh(inner)
    return 0.5 * (1.0 + hyper) + 0.5 * value * (1.0 - hyper * hyper) * 0.7978845608 * (
        1.0 + 3.0 * 0.044715 * value * value
    )


def body(fields, land, conv_in, conv_out, batchnorm_gain, batchnorm_offset, target_grad):
    lon, lat = (fields.shape[1], fields.shape[2])
    ocean_mask = land.astype(jnp.float32)[None, :, :, None]
    masked = fields * ocean_mask.astype(jnp.bfloat16)
    padded_in = surround(masked)
    first = convolve(padded_in, conv_in, lon, lat).astype(jnp.bfloat16)
    first_features = first.astype(jnp.float32)
    local_count = jnp.sum(land.astype(jnp.float32)) * fields.shape[0]
    sums, squares, element_count = lax.psum(
        (
            jnp.sum(first_features * ocean_mask, axis=(0, 1, 2)),
            jnp.sum(first_features * first_features * ocean_mask, axis=(0, 1, 2)),
            local_count,
        ),
        ("space", "batch"),
    )
    channel_mean = sums / element_count
    var = squares / element_count - channel_mean * channel_mean
    inverse_deviation = lax.rsqrt(var + 1e-05)
    normalized_input = (first_features - channel_mean) * inverse_deviation
    preactivation = batchnorm_gain * normalized_input + batchnorm_offset
    act = (gelu_value(preactivation) * ocean_mask).astype(jnp.bfloat16)
    padded_act = surround(act)
    output = (convolve(padded_act, conv_out, lon, lat) * ocean_mask).astype(jnp.bfloat16)
    dout = (target_grad.astype(jnp.float32) * ocean_mask * lax.rsqrt(element_count)).astype(
        jnp.bfloat16
    )
    grad_out = reduce_weights(tap_grads(padded_act, dout, lon, lat))
    dact = adjoint_conv(surround(dout), conv_out, lon, lat)
    preactivation_gradient = dact * ocean_mask * gelu_slope(preactivation)
    offset_gradient, gain_gradient = lax.psum(
        (
            jnp.sum(preactivation_gradient, axis=(0, 1, 2)),
            jnp.sum(preactivation_gradient * normalized_input, axis=(0, 1, 2)),
        ),
        ("space", "batch"),
    )
    first_layer_gradient = (
        ocean_mask
        * batchnorm_gain
        * inverse_deviation
        * (
            preactivation_gradient
            - (offset_gradient + normalized_input * gain_gradient) / element_count
        )
    ).astype(jnp.bfloat16)
    grad_in = reduce_weights(tap_grads(padded_in, first_layer_gradient, lon, lat))
    return (output, grad_in, grad_out, gain_gradient, offset_gradient)


def solution(mesh):
    in_specs = (
        P(("groups", "batch"), "space", None, None),
        P("space", None),
        P(),
        P(),
        P(),
        P(),
        P(("groups", "batch"), "space", None, None),
    )
    out_specs = (
        P(("groups", "batch"), "space", None, None),
        P("groups", None, "batch"),
        P("groups", None, "batch"),
        P("groups"),
        P("groups"),
    )
    return jax.shard_map(body, mesh=mesh, in_specs=in_specs, out_specs=out_specs, check_vma=False)
```

profile of v0, /device:TPU:0, one launch (start us, length us, event | category | flops | bytes accessed | tf_op | source)
XLA Modules:
  0.0 216.1 jit_solution(872169914859820042)
XLA Ops:
  7.2 0.7 fusion.202
  7.9 1.0 broadcast_multiply_fusion
  9.0 3.1 %collective-permute-start = (bf16[1,8,128]{2,1,0:T(8,128)(2,1)S(1)}, bf16[1,8,128]{2,1,0:T(8,128)(2,1)S(1)}, u32[]{:S(2)}, u32[]{:S(2)}) collective-permute-start(bf16[1,8,128]{2,1,0:T(8,128)(2,1)S(1)} %bitcast.514), channel_id=1, source_target_pairs={{0,4},{4,0},{8,12},{12,8},{1,5},{5,1},{9,13},{13,9},{2,6},{6,2},{1... | collective-permute-start | bytes 6152 | tf_op jit(solution)/shard_map/ppermute | solution.py:10
  12.1 1.6 collective-permute-done
  13.7 3.0 %collective-permute-start.1 = (bf16[1,8,128]{2,1,0:T(8,128)(2,1)S(1)}, bf16[1,8,128]{2,1,0:T(8,128)(2,1)S(1)}, u32[]{:S(2)}, u32[]{:S(2)}) collective-permute-start(bf16[1,8,128]{2,1,0:T(8,128)(2,1)S(1)} %collective-permute-done), channel_id=1, source_target_pairs={{0,8},{4,12},{8,0},{12,4},{1,9},{5,13},{9,1},{13,5},{2,10},{6,14},... | collective-permute-start | bytes 6152 | tf_op jit(solution)/shard_map/ppermute | solution.py:10
  17.4 0.9 collective-permute-done.1
  18.4 4.0 %collective-permute-start.3 = (bf16[1,1,66,128]{3,2,1,0:T(8,128)(2,1)S(1)}, bf16[1,1,66,128]{3,2,1,0:T(8,128)(2,1)S(1)}, u32[]{:S(2)}, u32[]{:S(2)}) collective-permute-start(bf16[1,1,66,128]{3,2,1,0:T(8,128)(2,1)S(1)} %get-tuple-element.94), channel_id=1, source_target_pairs={{4,0},{8,4},{12,8},{0,12},{5,1},{9,5},{13,9},{1,13},{6,2},{10,6},{... | collective-permute-start | bytes 50696 | tf_op jit(solution)/shard_map/ppermute | solution.py:21
  22.4 1.4 collective-permute-done.3
  23.8 4.1 %collective-permute-done.2 = bf16[1,1,66,128]{3,2,1,0:T(8,128)(2,1)S(1)} collective-permute-done((bf16[1,1,66,128]{3,2,1,0:T(8,128)(2,1)S(1)}, bf16[1,1,66,128]{3,2,1,0:T(8,128)(2,1)S(1)}, u32[]{:S(2)}, u32[]{:S(2)}) %collective-permute-start.2) | collective-permute-done | bytes 16928 | tf_op jit(solution)/shard_map/ppermute | solution.py:20
  28.2 0.8 copy-done.1
  30.6 30.1 %all-reduce.3 = (f32[]{:T(128)}, f32[128]{0:T(128)S(1)}, f32[128]{0:T(128)S(1)}) all-reduce(f32[]{:T(128)} %convert_reduce_fusion, f32[128]{0:T(128)S(1)} %get-tuple-element.55, f32[128]{0:T(128)S(1)} %get-tuple-element.54), channel_id=1, replica_groups=mesh['groups'=2,'space'=4,'batch'=4] {'space','batch'}, use_global_device_ids=true, to_apply=%region_3.4 | all-reduce | flops 257 | bytes 2056 | tf_op jit(solution)/shard_map/psum | solution.py:119
  61.7 3.6 %collective-permute-done.8 = bf16[1,8,128]{2,1,0:T(8,128)(2,1)S(1)} collective-permute-done((bf16[1,8,128]{2,1,0:T(8,128)(2,1)S(1)}, bf16[1,8,128]{2,1,0:T(8,128)(2,1)S(1)}, u32[]{:S(2)}, u32[]{:S(2)}) %collective-permute-start.8) | collective-permute-done | bytes 2080 | tf_op jit(solution)/shard_map/ppermute | solution.py:10
  65.3 4.5 %collective-permute-done.9 = bf16[1,8,128]{2,1,0:T(8,128)(2,1)S(1)} collective-permute-done((bf16[1,8,128]{2,1,0:T(8,128)(2,1)S(1)}, bf16[1,8,128]{2,1,0:T(8,128)(2,1)S(1)}, u32[]{:S(2)}, u32[]{:S(2)}) %collective-permute-start.9) | collective-permute-done | bytes 2080 | tf_op jit(solution)/shard_map/ppermute | solution.py:10
  69.9 2.0 collective-permute-start.10
  71.9 0.7 add_rsqrt_fusion
  72.6 1.1 collective-permute-done.11
  73.6 1.9 collective-permute-done.10
  75.9 0.7 copy-done
  78.9 0.6 copy-done.5
  80.1 3.4 %collective-permute-done.4 = bf16[1,8,128]{2,1,0:T(8,128)(2,1)S(1)} collective-permute-done((bf16[1,8,128]{2,1,0:T(8,128)(2,1)S(1)}, bf16[1,8,128]{2,1,0:T(8,128)(2,1)S(1)}, u32[]{:S(2)}, u32[]{:S(2)}) %collective-permute-start.4) | collective-permute-done | bytes 2080 | tf_op jit(solution)/shard_map/ppermute | solution.py:10
  83.6 29.5 %all-reduce.2 = (f32[128]{0:T(128)S(1)}, f32[128]{0:T(128)S(1)}) all-reduce(f32[128]{0:T(128)S(1)} %get-tuple-element.57, f32[128]{0:T(128)S(1)} %get-tuple-element.56), channel_id=1, replica_groups=mesh['groups'=2,'space'=4,'batch'=4] {'space','batch'}, use_global_device_ids=true, to_apply=%region_9.10 | all-reduce | flops 256 | bytes 2048 | tf_op jit(solution)/shard_map/psum | solution.py:141
  113.3 2.0 collective-permute-start.6
  115.4 1.7 collective-permute-done.7
  117.1 1.9 collective-permute-done.6
  121.0 1.5 multiply_convert_fusion
  124.7 1.2 copy.85
  128.0 1.2 copy.86
  129.3 15.8 %reduce-scatter.3.cloned.1.call-done = bf16[9,128,32]{1,0,2:T(8,128)(2,1)} async-done(((bf16[9,128,128]{1,0,2:T(8,128)(2,1)}), bf16[9,128,32]{1,0,2:T(8,128)(2,1)}) %reduce-scatter.3.cloned.1.call-update) | async-done | bytes 73744 | tf_op jit(solution)/shard_map/reduce_scatter | solution.py:95
  145.0 24.2 %reduce-scatter.5.cloned.1.call-done = bf16[9,128,32]{1,0,2:T(8,128)(2,1)} async-done(((bf16[9,128,128]{1,0,2:T(8,128)(2,1)}), bf16[9,128,32]{1,0,2:T(8,128)(2,1)}) %reduce-scatter.5.cloned.1.call-update) | async-done | bytes 73744 | tf_op jit(solution)/shard_map/reduce_scatter | solution.py:95
  169.2 38.1 %all-reduce.7.cloned.1.call-done = (bf16[9,128,32]{1,0,2:T(8,128)(2,1)}, bf16[9,128,32]{1,0,2:T(8,128)(2,1)}) async-done(((bf16[9,128,32]{1,0,2:T(8,128)(2,1)}, bf16[9,128,32]{1,0,2:T(8,128)(2,1)}), (bf16[9,128,32]{1,0,2:T(8,128)(2,1)}, bf16[9,128,32]{1,0,2:T(8,128)(2,1)})) %all-reduce.7.cloned.1.call-update) | async-done | bytes 147472 | tf_op jit(solution)/shard_map/psum | solution.py:94
  207.3 1.6 copy.87
  208.9 0.7 copy.88
  (116 shorter events, 12.8 us)
Async XLA Ops:
  7.2 137.9 %reduce-scatter.3.cloned.1.call-start = ((), (), s32[]{:S(2)}) async-start(), calls=%async_computation.2 | async-start | bytes 655360 | tf_op jit(solution)/shard_map/reduce_scatter | solution.py:95
  9.0 7.7 %copy-start.4 = (s32[8,64]{1,0:T(8,128)S(1)}, s32[8,64]{1,0:T(8,128)}, u32[]{:S(2)}) copy-start(s32[8,64]{1,0:T(8,128)} %param.12) | copy-start | bytes 6148
  9.0 4.7 %collective-permute-start = (bf16[1,8,128]{2,1,0:T(8,128)(2,1)S(1)}, bf16[1,8,128]{2,1,0:T(8,128)(2,1)S(1)}, u32[]{:S(2)}, u32[]{:S(2)}) collective-permute-start(bf16[1,8,128]{2,1,0:T(8,128)(2,1)S(1)} %bitcast.514), channel_id=1, source_target_pairs={{0,4},{4,0},{8,12},{12,8},{1,5},{5,1},{9,13},{13,9},{2,6},{6,2},{1... | collective-permute-start | bytes 6152 | tf_op jit(solution)/shard_map/ppermute | solution.py:10
  13.7 4.6 %collective-permute-start.1 = (bf16[1,8,128]{2,1,0:T(8,128)(2,1)S(1)}, bf16[1,8,128]{2,1,0:T(8,128)(2,1)S(1)}, u32[]{:S(2)}, u32[]{:S(2)}) collective-permute-start(bf16[1,8,128]{2,1,0:T(8,128)(2,1)S(1)} %collective-permute-done), channel_id=1, source_target_pairs={{0,8},{4,12},{8,0},{12,4},{1,9},{5,13},{9,1},{13,5},{2,10},{6,14},... | collective-permute-start | bytes 6152 | tf_op jit(solution)/shard_map/ppermute | solution.py:10
  18.4 5.5 %collective-permute-start.3 = (bf16[1,1,66,128]{3,2,1,0:T(8,128)(2,1)S(1)}, bf16[1,1,66,128]{3,2,1,0:T(8,128)(2,1)S(1)}, u32[]{:S(2)}, u32[]{:S(2)}) collective-permute-start(bf16[1,1,66,128]{3,2,1,0:T(8,128)(2,1)S(1)} %get-tuple-element.94), channel_id=1, source_target_pairs={{4,0},{8,4},{12,8},{0,12},{5,1},{9,5},{13,9},{1,13},{6,2},{10,6},{... | collective-permute-start | bytes 50696 | tf_op jit(solution)/shard_map/ppermute | solution.py:21
  22.4 5.6 %collective-permute-start.2 = (bf16[1,1,66,128]{3,2,1,0:T(8,128)(2,1)S(1)}, bf16[1,1,66,128]{3,2,1,0:T(8,128)(2,1)S(1)}, u32[]{:S(2)}, u32[]{:S(2)}) collective-permute-start(bf16[1,1,66,128]{3,2,1,0:T(8,128)(2,1)S(1)} %get-tuple-element.95), channel_id=1, source_target_pairs={{0,4},{4,8},{8,12},{12,0},{1,5},{5,9},{9,13},{13,1},{2,6},{6,10},{... | collective-permute-start | bytes 50696 | tf_op jit(solution)/shard_map/ppermute | solution.py:20
  28.0 1.0 copy-start.1
  30.4 31.1 %copy-start.2 = (bf16[1,8,64,128]{3,2,1,0:T(8,128)(2,1)S(1)}, bf16[1,8,64,128]{3,2,1,0:T(8,128)(2,1)}, u32[]{:S(2)}) copy-start(bf16[1,8,64,128]{3,2,1,0:T(8,128)(2,1)} %param.17) | copy-start | bytes 393220
  61.6 3.7 %collective-permute-start.8 = (bf16[1,8,128]{2,1,0:T(8,128)(2,1)S(1)}, bf16[1,8,128]{2,1,0:T(8,128)(2,1)S(1)}, u32[]{:S(2)}, u32[]{:S(2)}) collective-permute-start(bf16[1,8,128]{2,1,0:T(8,128)(2,1)S(1)} %bitcast.515), channel_id=1, source_target_pairs={{0,4},{4,0},{8,12},{12,8},{1,5},{5,1},{9,13},{13,9},{2,6},{6,2},{1... | collective-permute-start | bytes 6152 | tf_op jit(solution)/shard_map/ppermute | solution.py:10
  65.3 4.5 %collective-permute-start.9 = (bf16[1,8,128]{2,1,0:T(8,128)(2,1)S(1)}, bf16[1,8,128]{2,1,0:T(8,128)(2,1)S(1)}, u32[]{:S(2)}, u32[]{:S(2)}) collective-permute-start(bf16[1,8,128]{2,1,0:T(8,128)(2,1)S(1)} %collective-permute-done.8), channel_id=1, source_target_pairs={{0,8},{4,12},{8,0},{12,4},{1,9},{5,13},{9,1},{13,5},{2,10},{6,14},... | collective-permute-start | bytes 6152 | tf_op jit(solution)/shard_map/ppermute | solution.py:10
  69.8 3.8 %collective-permute-start.11 = (bf16[1,1,66,128]{3,2,1,0:T(8,128)(2,1)S(1)}, bf16[1,1,66,128]{3,2,1,0:T(8,128)(2,1)S(1)}, u32[]{:S(2)}, u32[]{:S(2)}) collective-permute-start(bf16[1,1,66,128]{3,2,1,0:T(8,128)(2,1)S(1)} %get-tuple-element.91), channel_id=1, source_target_pairs={{4,0},{8,4},{12,8},{0,12},{5,1},{9,5},{13,9},{1,13},{6,2},{10,6},{... | collective-permute-start | bytes 50696 | tf_op jit(solution)/shard_map/ppermute | solution.py:21
  69.9 5.6 %collective-permute-start.10 = (bf16[1,1,66,128]{3,2,1,0:T(8,128)(2,1)S(1)}, bf16[1,1,66,128]{3,2,1,0:T(8,128)(2,1)S(1)}, u32[]{:S(2)}, u32[]{:S(2)}) collective-permute-start(bf16[1,1,66,128]{3,2,1,0:T(8,128)(2,1)S(1)} %get-tuple-element.90), channel_id=1, source_target_pairs={{0,4},{4,8},{8,12},{12,0},{1,5},{5,9},{9,13},{13,1},{2,6},{6,10},{... | collective-permute-start | bytes 50696 | tf_op jit(solution)/shard_map/ppermute | solution.py:20
  75.7 1.0 copy-start
  78.9 0.7 copy-start.5
  78.9 0.7 copy-start.6
  79.8 3.7 %collective-permute-start.4 = (bf16[1,8,128]{2,1,0:T(8,128)(2,1)S(1)}, bf16[1,8,128]{2,1,0:T(8,128)(2,1)S(1)}, u32[]{:S(2)}, u32[]{:S(2)}) collective-permute-start(bf16[1,8,128]{2,1,0:T(8,128)(2,1)S(1)} %bitcast.516), channel_id=1, source_target_pairs={{0,4},{4,0},{8,12},{12,8},{1,5},{5,1},{9,13},{13,9},{2,6},{6,2},{1... | collective-permute-start | bytes 6152 | tf_op jit(solution)/shard_map/ppermute | solution.py:10
  83.5 29.6 %collective-permute-start.5 = (bf16[1,8,128]{2,1,0:T(8,128)(2,1)S(1)}, bf16[1,8,128]{2,1,0:T(8,128)(2,1)S(1)}, u32[]{:S(2)}, u32[]{:S(2)}) collective-permute-start(bf16[1,8,128]{2,1,0:T(8,128)(2,1)S(1)} %collective-permute-done.4), channel_id=1, source_target_pairs={{0,8},{4,12},{8,0},{12,4},{1,9},{5,13},{9,1},{13,5},{2,10},{6,14},... | collective-permute-start | bytes 6152 | tf_op jit(solution)/shard_map/ppermute | solution.py:10
  113.1 7.9 %copy-start.7 = (f32[128]{0:T(128)}, f32[128]{0:T(128)S(1)}, u32[]{:S(2)}) copy-start(f32[128]{0:T(128)S(1)} %get-tuple-element.58) | copy-start | bytes 1540
  113.1 7.9 %copy-start.8 = (f32[128]{0:T(128)}, f32[128]{0:T(128)S(1)}, u32[]{:S(2)}) copy-start(f32[128]{0:T(128)S(1)} %get-tuple-element.59) | copy-start | bytes 1540
  113.2 3.8 %collective-permute-start.7 = (bf16[1,1,66,128]{3,2,1,0:T(8,128)(2,1)S(1)}, bf16[1,1,66,128]{3,2,1,0:T(8,128)(2,1)S(1)}, u32[]{:S(2)}, u32[]{:S(2)}) collective-permute-start(bf16[1,1,66,128]{3,2,1,0:T(8,128)(2,1)S(1)} %get-tuple-element.92), channel_id=1, source_target_pairs={{4,0},{8,4},{12,8},{0,12},{5,1},{9,5},{13,9},{1,13},{6,2},{10,6},{... | collective-permute-start | bytes 50696 | tf_op jit(solution)/shard_map/ppermute | solution.py:21
  113.3 5.6 %collective-permute-start.6 = (bf16[1,1,66,128]{3,2,1,0:T(8,128)(2,1)S(1)}, bf16[1,1,66,128]{3,2,1,0:T(8,128)(2,1)S(1)}, u32[]{:S(2)}, u32[]{:S(2)}) collective-permute-start(bf16[1,1,66,128]{3,2,1,0:T(8,128)(2,1)S(1)} %get-tuple-element.93), channel_id=1, source_target_pairs={{0,4},{4,8},{8,12},{12,0},{1,5},{5,9},{9,13},{13,1},{2,6},{6,10},{... | collective-permute-start | bytes 50696 | tf_op jit(solution)/shard_map/ppermute | solution.py:20
  125.9 43.3 %reduce-scatter.5.cloned.1.call-start = ((), (), s32[]{:S(2)}) async-start(), calls=%async_computation.3 | async-start | bytes 655360 | tf_op jit(solution)/shard_map/reduce_scatter | solution.py:95
  129.2 78.1 %all-reduce.7.cloned.1.call-start = ((), (), s32[]{:S(2)}) async-start(), calls=%async_computation.4 | async-start | bytes 524288 | tf_op jit(solution)/shard_map/psum | solution.py:94
  207.3 1.6 copy-start.3
Sparse Core Ops, SparseCore 0:
  126.0 18.9 reduce-scatter.2
  147.5 21.6 reduce-scatter.4
  171.6 35.6 all-reduce.6
where the time goes:
time: 216 us
  waiting for transfers between devices  104 us (48%)
  blocking collectives  59.6 us (28%)
  between operations  15 us (7%)
  starting transfers between devices  14.7 us (7%)
  matrix products  9.6 us (4%)
  local copies, waits for them, and re-layouts  7.76 us (4%)
  other arithmetic  5.5 us (3%)
    reduce_scatter x2, waiting for transfers between devices, reduce_weights(): lax.psum_scatter(summed, 'batch', scatter_dimension=2, tiled=True)  39.9 us
    psum x1, waiting for transfers between devices, reduce_weights(): summed = lax.psum(partial_grad.astype(jnp.bfloat16), 'space')  38.1 us
    psum x1, blocking collectives, body(): lax.psum((jnp.sum(first_features * ocean_mask, axis=(0, 1, 2)), jnp.sum(f...  30.1 us
    psum x1, blocking collectives, body(): lax.psum((jnp.sum(preactivation_gradient, axis=(0, 1, 2)), jnp.sum(preact...  29.5 us
    ppermute x6, waiting for transfers between devices, partner(): return lax.ppermute(value, axis, pairs)  13.9 us
    ppermute x3, waiting for transfers between devices, extended_2(): before = lax.ppermute(last, axis, up)  7.82 us
    ppermute x6, starting transfers between devices, partner(): return lax.ppermute(value, axis, pairs)  6.46 us
    unnamed x24, local copies, waits for them, and re-layouts  4.49 us
  transfers between devices with their start and end apart: 15, of which 14 were waited for; matrix products, arithmetic and copies ran while one was open for 2% of the time, Pallas kernels for 0%

commit v1 on v0

--- a/solution.py
+++ b/solution.py
@@ -2,6 +2,11 @@
 import jax.numpy as jnp
 from jax import lax
 from jax.sharding import PartitionSpec as P
+
+
+def axis_by_axis(array, leading, second_2):
+    half = lax.psum(array, leading)
+    return lax.psum(half, second_2)
 
 
 def partner(value, axis, distance):
@@ -138,12 +143,13 @@
     grad_out = reduce_weights(tap_grads(padded_act, dout, lon, lat))
     dact = adjoint_conv(surround(dout), conv_out, lon, lat)
     preactivation_gradient = dact * ocean_mask * gelu_slope(preactivation)
-    offset_gradient, gain_gradient = lax.psum(
+    offset_gradient, gain_gradient = axis_by_axis(
         (
             jnp.sum(preactivation_gradient, axis=(0, 1, 2)),
             jnp.sum(preactivation_gradient * normalized_input, axis=(0, 1, 2)),
         ),
-        ("space", "batch"),
+        "batch",
+        "space",
     )
     first_layer_gradient = (
         ocean_mask

time: 216 us -> 204 us (0.944)
  blocking collectives: 59.6 us -> 46.8 us
    psum x1 -> x2, blocking collectives: 29.5 us -> 16.6 us  [the longest x1 10.9 us: axis_by_axis(): return lax.psum(half, second_2)]
where the time goes in v1:
time: 204 us; the launch traced here: 203 us
  waiting for transfers between devices  104 us (51%)
  blocking collectives  46.8 us (23%)
  between operations  15 us (7%)
  starting transfers between devices  14.7 us (7%)
  matrix products  9.59 us (5%)
  local copies, waits for them, and re-layouts  7.79 us (4%)
  other arithmetic  5.5 us (3%)
    reduce_scatter x2, waiting for transfers between devices, reduce_weights(): lax.psum_scatter(summed, 'batch', scatter_dimension=2, tiled=True)  39.9 us
    psum x1, waiting for transfers between devices, reduce_weights(): summed = lax.psum(partial_grad.astype(jnp.bfloat16), 'space')  38 us
    psum x1, blocking collectives, body(): lax.psum((jnp.sum(first_features * ocean_mask, axis=(0, 1, 2)), jnp.sum(f...  30.1 us
    ppermute x6, waiting for transfers between devices, partner(): return lax.ppermute(value, axis, pairs)  13.9 us
    psum x1, blocking collectives, axis_by_axis(): return lax.psum(half, second_2)  10.9 us
    ppermute x3, waiting for transfers between devices, extended_2(): before = lax.ppermute(last, axis, up)  7.82 us
    ppermute x6, starting transfers between devices, partner(): return lax.ppermute(value, axis, pairs)  6.46 us
    psum x1, blocking collectives, axis_by_axis(): half = lax.psum(array, leading)  5.76 us
  transfers between devices with their start and end apart: 15, of which 14 were waited for; matrix products, arithmetic and copies ran while one was open for 2% of the time, Pallas kernels for 0%

profile of v1, /device:TPU:0, one launch (start us, length us, event | category | flops | bytes accessed | tf_op | source)
XLA Modules:
  0.0 203.3 jit_solution(1629398224299975106)
XLA Ops:
  7.2 0.7 fusion.202
  7.9 1.0 broadcast_multiply_fusion
  9.0 3.1 %collective-permute-start = (bf16[1,8,128]{2,1,0:T(8,128)(2,1)S(1)}, bf16[1,8,128]{2,1,0:T(8,128)(2,1)S(1)}, u32[]{:S(2)}, u32[]{:S(2)}) collective-permute-start(bf16[1,8,128]{2,1,0:T(8,128)(2,1)S(1)} %bitcast.514), channel_id=1, source_target_pairs={{0,4},{4,0},{8,12},{12,8},{1,5},{5,1},{9,13},{13,9},{2,6},{6,2},{1... | collective-permute-start | bytes 6152 | tf_op jit(solution)/shard_map/ppermute | solution.py:15
  12.1 1.6 collective-permute-done
  13.7 3.0 %collective-permute-start.1 = (bf16[1,8,128]{2,1,0:T(8,128)(2,1)S(1)}, bf16[1,8,128]{2,1,0:T(8,128)(2,1)S(1)}, u32[]{:S(2)}, u32[]{:S(2)}) collective-permute-start(bf16[1,8,128]{2,1,0:T(8,128)(2,1)S(1)} %collective-permute-done), channel_id=1, source_target_pairs={{0,8},{4,12},{8,0},{12,4},{1,9},{5,13},{9,1},{13,5},{2,10},{6,14},... | collective-permute-start | bytes 6152 | tf_op jit(solution)/shard_map/ppermute | solution.py:15
  17.4 0.9 collective-permute-done.1
  18.4 4.0 %collective-permute-start.3 = (bf16[1,1,66,128]{3,2,1,0:T(8,128)(2,1)S(1)}, bf16[1,1,66,128]{3,2,1,0:T(8,128)(2,1)S(1)}, u32[]{:S(2)}, u32[]{:S(2)}) collective-permute-start(bf16[1,1,66,128]{3,2,1,0:T(8,128)(2,1)S(1)} %get-tuple-element.96), channel_id=1, source_target_pairs={{4,0},{8,4},{12,8},{0,12},{5,1},{9,5},{13,9},{1,13},{6,2},{10,6},{... | collective-permute-start | bytes 50696 | tf_op jit(solution)/shard_map/ppermute | solution.py:26
  22.4 1.4 collective-permute-done.3
  23.8 4.1 %collective-permute-done.2 = bf16[1,1,66,128]{3,2,1,0:T(8,128)(2,1)S(1)} collective-permute-done((bf16[1,1,66,128]{3,2,1,0:T(8,128)(2,1)S(1)}, bf16[1,1,66,128]{3,2,1,0:T(8,128)(2,1)S(1)}, u32[]{:S(2)}, u32[]{:S(2)}) %collective-permute-start.2) | collective-permute-done | bytes 16928 | tf_op jit(solution)/shard_map/ppermute | solution.py:25
  28.2 0.8 copy-done.1
  30.6 30.1 %all-reduce.2 = (f32[]{:T(128)}, f32[128]{0:T(128)S(1)}, f32[128]{0:T(128)S(1)}) all-reduce(f32[]{:T(128)} %convert_reduce_fusion, f32[128]{0:T(128)S(1)} %get-tuple-element.55, f32[128]{0:T(128)S(1)} %get-tuple-element.54), channel_id=1, replica_groups=mesh['groups'=2,'space'=4,'batch'=4] {'space','batch'}, use_global_device_ids=true, to_apply=%region_3.4 | all-reduce | flops 257 | bytes 2056 | tf_op jit(solution)/shard_map/psum | solution.py:124
  61.7 3.6 %collective-permute-done.8 = bf16[1,8,128]{2,1,0:T(8,128)(2,1)S(1)} collective-permute-done((bf16[1,8,128]{2,1,0:T(8,128)(2,1)S(1)}, bf16[1,8,128]{2,1,0:T(8,128)(2,1)S(1)}, u32[]{:S(2)}, u32[]{:S(2)}) %collective-permute-start.8) | collective-permute-done | bytes 2080 | tf_op jit(solution)/shard_map/ppermute | solution.py:15
  65.3 4.5 %collective-permute-done.9 = bf16[1,8,128]{2,1,0:T(8,128)(2,1)S(1)} collective-permute-done((bf16[1,8,128]{2,1,0:T(8,128)(2,1)S(1)}, bf16[1,8,128]{2,1,0:T(8,128)(2,1)S(1)}, u32[]{:S(2)}, u32[]{:S(2)}) %collective-permute-start.9) | collective-permute-done | bytes 2080 | tf_op jit(solution)/shard_map/ppermute | solution.py:15
  69.9 2.0 collective-permute-start.10
  71.9 0.7 add_rsqrt_fusion
  72.6 1.1 collective-permute-done.11
  73.6 1.9 collective-permute-done.10
  75.9 0.7 copy-done
  80.1 3.4 %collective-permute-done.4 = bf16[1,8,128]{2,1,0:T(8,128)(2,1)S(1)} collective-permute-done((bf16[1,8,128]{2,1,0:T(8,128)(2,1)S(1)}, bf16[1,8,128]{2,1,0:T(8,128)(2,1)S(1)}, u32[]{:S(2)}, u32[]{:S(2)}) %collective-permute-start.4) | collective-permute-done | bytes 2080 | tf_op jit(solution)/shard_map/ppermute | solution.py:15
  83.6 5.8 %all-reduce.3 = (f32[128]{0:T(128)S(1)}, f32[128]{0:T(128)S(1)}) all-reduce(f32[128]{0:T(128)S(1)} %get-tuple-element.57, f32[128]{0:T(128)S(1)} %get-tuple-element.56), channel_id=1, replica_groups=mesh['groups'=2,'space'=4,'batch'=4] {'batch'}, use_global_device_ids=true, to_apply=%region_10.11 | all-reduce | flops 256 | bytes 2048 | tf_op jit(solution)/shard_map/psum | solution.py:8
  89.4 10.9 %all-reduce.4 = (f32[128]{0:T(128)S(1)}, f32[128]{0:T(128)S(1)}) all-reduce(f32[128]{0:T(128)S(1)} %get-tuple-element.61, f32[128]{0:T(128)S(1)} %get-tuple-element.62), channel_id=1, replica_groups=mesh['groups'=2,'space'=4,'batch'=4] {'space'}, use_global_device_ids=true, to_apply=%region_11.12 | all-reduce | flops 256 | bytes 2048 | tf_op jit(solution)/shard_map/psum | solution.py:9
  100.5 2.0 collective-permute-start.6
  102.5 1.7 collective-permute-done.7
  104.2 1.9 collective-permute-done.6
  108.1 1.5 multiply_convert_fusion
  111.8 1.2 copy.85
  115.1 1.2 copy.86
  116.4 15.8 %reduce-scatter.3.cloned.1.call-done = bf16[9,128,32]{1,0,2:T(8,128)(2,1)} async-done(((bf16[9,128,128]{1,0,2:T(8,128)(2,1)}), bf16[9,128,32]{1,0,2:T(8,128)(2,1)}) %reduce-scatter.3.cloned.1.call-update) | async-done | bytes 73744 | tf_op jit(solution)/shard_map/reduce_scatter | solution.py:100
  132.2 24.2 %reduce-scatter.5.cloned.1.call-done = bf16[9,128,32]{1,0,2:T(8,128)(2,1)} async-done(((bf16[9,128,128]{1,0,2:T(8,128)(2,1)}), bf16[9,128,32]{1,0,2:T(8,128)(2,1)}) %reduce-scatter.5.cloned.1.call-update) | async-done | bytes 73744 | tf_op jit(solution)/shard_map/reduce_scatter | solution.py:100
  156.4 38.0 %all-reduce.8.cloned.1.call-done = (bf16[9,128,32]{1,0,2:T(8,128)(2,1)}, bf16[9,128,32]{1,0,2:T(8,128)(2,1)}) async-done(((bf16[9,128,32]{1,0,2:T(8,128)(2,1)}, bf16[9,128,32]{1,0,2:T(8,128)(2,1)}), (bf16[9,128,32]{1,0,2:T(8,128)(2,1)}, bf16[9,128,32]{1,0,2:T(8,128)(2,1)})) %all-reduce.8.cloned.1.call-update) | async-done | bytes 147472 | tf_op jit(solution)/shard_map/psum | solution.py:99
  194.4 1.6 copy.87
  196.0 0.7 copy.88
  (117 shorter events, 13.5 us)
Async XLA Ops:
  7.2 125.0 %reduce-scatter.3.cloned.1.call-start = ((), (), s32[]{:S(2)}) async-start(), calls=%async_computation.2 | async-start | bytes 655360 | tf_op jit(solution)/shard_map/reduce_scatter | solution.py:100
  9.0 7.7 %copy-start.4 = (s32[8,64]{1,0:T(8,128)S(1)}, s32[8,64]{1,0:T(8,128)}, u32[]{:S(2)}) copy-start(s32[8,64]{1,0:T(8,128)} %param.12) | copy-start | bytes 6148
  9.0 4.7 %collective-permute-start = (bf16[1,8,128]{2,1,0:T(8,128)(2,1)S(1)}, bf16[1,8,128]{2,1,0:T(8,128)(2,1)S(1)}, u32[]{:S(2)}, u32[]{:S(2)}) collective-permute-start(bf16[1,8,128]{2,1,0:T(8,128)(2,1)S(1)} %bitcast.514), channel_id=1, source_target_pairs={{0,4},{4,0},{8,12},{12,8},{1,5},{5,1},{9,13},{13,9},{2,6},{6,2},{1... | collective-permute-start | bytes 6152 | tf_op jit(solution)/shard_map/ppermute | solution.py:15
  13.7 4.6 %collective-permute-start.1 = (bf16[1,8,128]{2,1,0:T(8,128)(2,1)S(1)}, bf16[1,8,128]{2,1,0:T(8,128)(2,1)S(1)}, u32[]{:S(2)}, u32[]{:S(2)}) collective-permute-start(bf16[1,8,128]{2,1,0:T(8,128)(2,1)S(1)} %collective-permute-done), channel_id=1, source_target_pairs={{0,8},{4,12},{8,0},{12,4},{1,9},{5,13},{9,1},{13,5},{2,10},{6,14},... | collective-permute-start | bytes 6152 | tf_op jit(solution)/shard_map/ppermute | solution.py:15
  18.4 5.5 %collective-permute-start.3 = (bf16[1,1,66,128]{3,2,1,0:T(8,128)(2,1)S(1)}, bf16[1,1,66,128]{3,2,1,0:T(8,128)(2,1)S(1)}, u32[]{:S(2)}, u32[]{:S(2)}) collective-permute-start(bf16[1,1,66,128]{3,2,1,0:T(8,128)(2,1)S(1)} %get-tuple-element.96), channel_id=1, source_target_pairs={{4,0},{8,4},{12,8},{0,12},{5,1},{9,5},{13,9},{1,13},{6,2},{10,6},{... | collective-permute-start | bytes 50696 | tf_op jit(solution)/shard_map/ppermute | solution.py:26
  22.4 5.6 %collective-permute-start.2 = (bf16[1,1,66,128]{3,2,1,0:T(8,128)(2,1)S(1)}, bf16[1,1,66,128]{3,2,1,0:T(8,128)(2,1)S(1)}, u32[]{:S(2)}, u32[]{:S(2)}) collective-permute-start(bf16[1,1,66,128]{3,2,1,0:T(8,128)(2,1)S(1)} %get-tuple-element.97), channel_id=1, source_target_pairs={{0,4},{4,8},{8,12},{12,0},{1,5},{5,9},{9,13},{13,1},{2,6},{6,10},{... | collective-permute-start | bytes 50696 | tf_op jit(solution)/shard_map/ppermute | solution.py:25
  28.0 1.0 copy-start.1
  30.4 31.1 %copy-start.2 = (bf16[1,8,64,128]{3,2,1,0:T(8,128)(2,1)S(1)}, bf16[1,8,64,128]{3,2,1,0:T(8,128)(2,1)}, u32[]{:S(2)}) copy-start(bf16[1,8,64,128]{3,2,1,0:T(8,128)(2,1)} %param.17) | copy-start | bytes 393220
  61.6 3.7 %collective-permute-start.8 = (bf16[1,8,128]{2,1,0:T(8,128)(2,1)S(1)}, bf16[1,8,128]{2,1,0:T(8,128)(2,1)S(1)}, u32[]{:S(2)}, u32[]{:S(2)}) collective-permute-start(bf16[1,8,128]{2,1,0:T(8,128)(2,1)S(1)} %bitcast.515), channel_id=1, source_target_pairs={{0,4},{4,0},{8,12},{12,8},{1,5},{5,1},{9,13},{13,9},{2,6},{6,2},{1... | collective-permute-start | bytes 6152 | tf_op jit(solution)/shard_map/ppermute | solution.py:15
  65.3 4.5 %collective-permute-start.9 = (bf16[1,8,128]{2,1,0:T(8,128)(2,1)S(1)}, bf16[1,8,128]{2,1,0:T(8,128)(2,1)S(1)}, u32[]{:S(2)}, u32[]{:S(2)}) collective-permute-start(bf16[1,8,128]{2,1,0:T(8,128)(2,1)S(1)} %collective-permute-done.8), channel_id=1, source_target_pairs={{0,8},{4,12},{8,0},{12,4},{1,9},{5,13},{9,1},{13,5},{2,10},{6,14},... | collective-permute-start | bytes 6152 | tf_op jit(solution)/shard_map/ppermute | solution.py:15
  69.8 3.8 %collective-permute-start.11 = (bf16[1,1,66,128]{3,2,1,0:T(8,128)(2,1)S(1)}, bf16[1,1,66,128]{3,2,1,0:T(8,128)(2,1)S(1)}, u32[]{:S(2)}, u32[]{:S(2)}) collective-permute-start(bf16[1,1,66,128]{3,2,1,0:T(8,128)(2,1)S(1)} %get-tuple-element.93), channel_id=1, source_target_pairs={{4,0},{8,4},{12,8},{0,12},{5,1},{9,5},{13,9},{1,13},{6,2},{10,6},{... | collective-permute-start | bytes 50696 | tf_op jit(solution)/shard_map/ppermute | solution.py:26
  69.9 5.6 %collective-permute-start.10 = (bf16[1,1,66,128]{3,2,1,0:T(8,128)(2,1)S(1)}, bf16[1,1,66,128]{3,2,1,0:T(8,128)(2,1)S(1)}, u32[]{:S(2)}, u32[]{:S(2)}) collective-permute-start(bf16[1,1,66,128]{3,2,1,0:T(8,128)(2,1)S(1)} %get-tuple-element.92), channel_id=1, source_target_pairs={{0,4},{4,8},{8,12},{12,0},{1,5},{5,9},{9,13},{13,1},{2,6},{6,10},{... | collective-permute-start | bytes 50696 | tf_op jit(solution)/shard_map/ppermute | solution.py:25
  75.7 1.0 copy-start
  78.9 0.7 copy-start.5
  78.9 0.7 copy-start.6
  79.8 3.7 %collective-permute-start.4 = (bf16[1,8,128]{2,1,0:T(8,128)(2,1)S(1)}, bf16[1,8,128]{2,1,0:T(8,128)(2,1)S(1)}, u32[]{:S(2)}, u32[]{:S(2)}) collective-permute-start(bf16[1,8,128]{2,1,0:T(8,128)(2,1)S(1)} %bitcast.516), channel_id=1, source_target_pairs={{0,4},{4,0},{8,12},{12,8},{1,5},{5,1},{9,13},{13,9},{2,6},{6,2},{1... | collective-permute-start | bytes 6152 | tf_op jit(solution)/shard_map/ppermute | solution.py:15
  83.5 16.8 %collective-permute-start.5 = (bf16[1,8,128]{2,1,0:T(8,128)(2,1)S(1)}, bf16[1,8,128]{2,1,0:T(8,128)(2,1)S(1)}, u32[]{:S(2)}, u32[]{:S(2)}) collective-permute-start(bf16[1,8,128]{2,1,0:T(8,128)(2,1)S(1)} %collective-permute-done.4), channel_id=1, source_target_pairs={{0,8},{4,12},{8,0},{12,4},{1,9},{5,13},{9,1},{13,5},{2,10},{6,14},... | collective-permute-start | bytes 6152 | tf_op jit(solution)/shard_map/ppermute | solution.py:15
  100.3 7.9 %copy-start.7 = (f32[128]{0:T(128)}, f32[128]{0:T(128)S(1)}, u32[]{:S(2)}) copy-start(f32[128]{0:T(128)S(1)} %get-tuple-element.63) | copy-start | bytes 1540
  100.3 7.9 %copy-start.8 = (f32[128]{0:T(128)}, f32[128]{0:T(128)S(1)}, u32[]{:S(2)}) copy-start(f32[128]{0:T(128)S(1)} %get-tuple-element.64) | copy-start | bytes 1540
  100.4 3.8 %collective-permute-start.7 = (bf16[1,1,66,128]{3,2,1,0:T(8,128)(2,1)S(1)}, bf16[1,1,66,128]{3,2,1,0:T(8,128)(2,1)S(1)}, u32[]{:S(2)}, u32[]{:S(2)}) collective-permute-start(bf16[1,1,66,128]{3,2,1,0:T(8,128)(2,1)S(1)} %get-tuple-element.94), channel_id=1, source_target_pairs={{4,0},{8,4},{12,8},{0,12},{5,1},{9,5},{13,9},{1,13},{6,2},{10,6},{... | collective-permute-start | bytes 50696 | tf_op jit(solution)/shard_map/ppermute | solution.py:26
  100.5 5.6 %collective-permute-start.6 = (bf16[1,1,66,128]{3,2,1,0:T(8,128)(2,1)S(1)}, bf16[1,1,66,128]{3,2,1,0:T(8,128)(2,1)S(1)}, u32[]{:S(2)}, u32[]{:S(2)}) collective-permute-start(bf16[1,1,66,128]{3,2,1,0:T(8,128)(2,1)S(1)} %get-tuple-element.95), channel_id=1, source_target_pairs={{0,4},{4,8},{8,12},{12,0},{1,5},{5,9},{9,13},{13,1},{2,6},{6,10},{... | collective-permute-start | bytes 50696 | tf_op jit(solution)/shard_map/ppermute | solution.py:25
  113.1 43.3 %reduce-scatter.5.cloned.1.call-start = ((), (), s32[]{:S(2)}) async-start(), calls=%async_computation.3 | async-start | bytes 655360 | tf_op jit(solution)/shard_map/reduce_scatter | solution.py:100
  116.4 78.1 %all-reduce.8.cloned.1.call-start = ((), (), s32[]{:S(2)}) async-start(), calls=%async_computation.4 | async-start | bytes 524288 | tf_op jit(solution)/shard_map/psum | solution.py:99
  194.4 1.6 copy-start.3
Sparse Core Ops, SparseCore 0:
  113.2 18.9 reduce-scatter.2
  134.7 21.6 reduce-scatter.4
  158.7 35.6 all-reduce.7
